TPU v7x, 256 devices: a whole 4x4x8 slice. The times are simulated.
256 devices in a mesh: dp: 32 (over x, z), feat: 8 (over y, core).
Axes of the slice: x: 4, y: 4, z: 8, core: 2. Of those that a mesh axis runs over, the one named last changes fastest.
Arguments:
- hidden_first: bfloat16 [2048, 4096], P('dp', 'feat'), may hold values from -6 to 6
- hidden_second: bfloat16 [2048, 4096], P('dp', 'feat'), may hold values from -11 to 11
- weight: bfloat16 [4096, 8192], P('dp', 'feat'), may hold values from -0.09375 to 0.09375
Outputs:
- total_loss: float32 [], replicated
- grad_weight: bfloat16 [4096, 8192], P('dp', 'feat')
- grad_first: bfloat16 [2048, 4096], P('dp', 'feat')
- grad_second: bfloat16 [2048, 4096], P('dp', 'feat')
All inputs are finite; a program needn't handle non-finite values.
Results may differ from a plain program's by a relative error of at most 0.015.
Values may be sent and summed in bfloat16 or wider, within the bound.
No kernel may reach another device: no remote copies, remote signals or barrier semaphores. Data moves between devices by JAX's collectives and lax.ppermute only.
A program may use at most 64 MiB of HBM per device.

v0:
```python
import jax
import jax.numpy as jnp
from jax import lax
from jax.sharding import PartitionSpec as P


def on_device(hidden_first, hidden_second, weight):
    dp_size = lax.axis_size("dp")
    feat_size = lax.axis_size("feat")
    row_count = hidden_first.shape[0]
    col_count = weight.shape[1]
    total_rows = row_count * dp_size * 1.0
    full_width = col_count * feat_size * 1.0
    full_first, full_second = (
        lax.all_gather(hidden_first, "feat", axis=1, tiled=True),
        lax.all_gather(hidden_second, "feat", axis=1, tiled=True),
    )
    stacked = jnp.concatenate([full_first, full_second], axis=0)
    whole_weight = lax.all_gather(weight, "dp", axis=0, tiled=True)
    outputs = jnp.dot(stacked, whole_weight, preferred_element_type=jnp.float32)
    views = outputs.reshape(2, row_count, col_count)
    col_sum = lax.psum(jnp.sum(views, axis=1), "dp")
    col_mean = col_sum / total_rows
    centered = views - col_mean[:, None, :]
    second_sum = lax.psum(jnp.sum(centered * centered, axis=1), "dp")
    variance = second_sum / (total_rows - 1.0)
    deviation = jnp.sqrt(variance + 0.0001)
    centered_half = centered.astype(jnp.bfloat16)
    gathered = lax.all_gather(centered_half, "dp", axis=1, tiled=True)
    gram_part = jnp.einsum(
        "vrc,vnc->vrn", centered_half, gathered, preferred_element_type=jnp.float32
    )
    gram_rows = lax.psum(gram_part.astype(jnp.bfloat16), "feat").astype(jnp.float32)
    gram_half = gram_rows.astype(jnp.bfloat16)
    spread = jnp.einsum("vrn,vnc->vrc", gram_half, gathered, preferred_element_type=jnp.float32)
    difference = views[0] - views[1]
    local_share = (
        25.0 * jnp.sum(difference * difference) / (total_rows * full_width)
        + 25.0 * jnp.sum(jax.nn.relu(1.0 - deviation)) / (full_width * dp_size)
        + (
            jnp.sum(gram_rows * gram_rows) / ((total_rows - 1.0) ** 2 * feat_size)
            - jnp.sum(variance * variance) / dp_size
        )
        / full_width
    )
    total_loss = lax.psum(local_share, ("dp", "feat"))
    inv_grad = 50.0 / 256.0 * jnp.stack([difference, -difference])
    binding = (deviation < 1.0).astype(jnp.float32)
    hinge_grad = (
        -(25.0 * total_rows / (256.0 * (total_rows - 1.0)))
        * (binding / deviation)[:, None, :]
        * centered
    )
    cov_grad = (
        4.0
        * total_rows
        / 256.0
        * (spread / (total_rows - 1.0) ** 2 - variance[:, None, :] * centered / (total_rows - 1.0))
    )
    grad_views = (inv_grad + hinge_grad + cov_grad).astype(jnp.bfloat16)
    flat_grads = grad_views.reshape(2 * row_count, col_count)
    input_terms = lax.dot_general(
        flat_grads, whole_weight, (((1,), (1,)), ((), ())), preferred_element_type=jnp.float32
    )
    input_grads = lax.psum_scatter(
        input_terms.astype(jnp.bfloat16), "feat", scatter_dimension=1, tiled=True
    )
    grad_first = input_grads[:row_count]
    grad_second = input_grads[row_count:]
    grad_weight = lax.psum_scatter(
        lax.dot_general(
            stacked, flat_grads, (((0,), (0,)), ((), ())), preferred_element_type=jnp.float32
        ).astype(jnp.bfloat16),
        "dp",
        scatter_dimension=0,
        tiled=True,
    )
    return (total_loss, grad_weight, grad_first, grad_second)


def solution(mesh):
    placed = (P("dp", "feat"), P("dp", "feat"), P("dp", "feat"))
    return jax.shard_map(
        on_device,
        mesh=mesh,
        in_specs=placed,
        out_specs=(P(), P("dp", "feat"), P("dp", "feat"), P("dp", "feat")),
        check_vma=False,
    )
```

profile of v0, /device:TPU:8, one launch (start us, length us, event | category | flops | bytes accessed | tf_op | source)
XLA Modules:
  0.0 638.5 jit_solution(8527642386405286671)
XLA Ops:
  7.2 0.0 all-gather.3.cloned.1.call-start
  7.2 0.7 all-gather.3.cloned.1.call-update
  7.9 0.0 all-gather.5.cloned.1.call-start
  7.9 13.5 %all_gather.12 = bf16[64,4096]{1,0:T(8,128)(2,1)S(1)} all-gather(bf16[64,512]{1,0:T(8,128)(2,1)} %param.3), channel_id=1, replica_groups=mesh['dp'=32,'feat'=8] {'feat'}, dimensions={1}, use_global_device_ids=true | all-gather | bytes 589824 | tf_op jit(solution)/shard_map/all_gather | solution.py:15
  21.5 13.3 %all_gather.13 = bf16[64,4096]{1,0:T(8,128)(2,1)S(1)} all-gather(bf16[64,512]{1,0:T(8,128)(2,1)} %param.4), channel_id=1, replica_groups=mesh['dp'=32,'feat'=8] {'feat'}, dimensions={1}, use_global_device_ids=true | all-gather | bytes 589824 | tf_op jit(solution)/shard_map/all_gather | solution.py:16
  34.9 76.4 %all-gather.3.cloned.1.call-done = bf16[4096,1024]{1,0:T(8,128)(2,1)} async-done(((bf16[128,1024]{1,0:T(8,128)(2,1)}), bf16[4096,1024]{1,0:T(8,128)(2,1)}) %all-gather.3.cloned.1.call-update) | async-done | bytes 8388624 | tf_op jit(solution)/shard_map/all_gather | solution.py:19
  111.3 4.7 bitcast_reduce_fusion
  115.9 72.4 %psum.28 = f32[2,1024]{1,0:T(2,128)S(1)} all-reduce(f32[2,1024]{1,0:T(2,128)S(1)} %get-tuple-element.15), channel_id=1, replica_groups=mesh['dp'=32,'feat'=8] {'dp'}, use_global_device_ids=true, to_apply=%region_2.0 | all-reduce | flops 2048 | bytes 16384 | tf_op jit(solution)/shard_map/psum | solution.py:22
  188.3 0.8 fusion.5
  189.1 0.0 all-gather.5.cloned.1.call-update
  189.1 0.0 all-reduce.2.cloned.1.call-start
  189.2 72.3 %psum.29 = f32[2,1024]{1,0:T(2,128)S(1)} all-reduce(f32[2,1024]{1,0:T(2,128)S(1)} %get-tuple-element.7), channel_id=1, replica_groups=mesh['dp'=32,'feat'=8] {'dp'}, use_global_device_ids=true, to_apply=%region_4.0 | all-reduce | flops 2048 | bytes 16384 | tf_op jit(solution)/shard_map/psum | solution.py:25
  261.4 19.3 %all-gather.5.cloned.1.call-done = bf16[2,2048,1024]{2,1,0:T(8,128)(2,1)} async-done(((bf16[2,64,1024]{2,1,0:T(8,128)(2,1)}), bf16[2,2048,1024]{2,1,0:T(8,128)(2,1)}) %all-gather.5.cloned.1.call-update) | async-done | bytes 8388624 | tf_op jit(solution)/shard_map/all_gather | solution.py:29
  280.8 6.9 %convolution_convert_fusion.2 = bf16[2,64,2048]{2,1,0:T(8,128)(2,1)} fusion(bf16[2,64,1024]{2,1,0:T(8,128)(2,1)} %get-tuple-element.6, bf16[2,2048,1024]{2,1,0:T(8,128)(2,1)} %all-gather.5.cloned.1.call-done), kind=kOutput, calls=%fused_computation.2 | convolution fusion | flops 537133056 | bytes 9175040 | tf_op jit(solution)/shard_map/vrc,vnc->vrn/dot_general | solution.py:30
  287.7 0.0 all-reduce.2.cloned.1.call-update
  287.8 0.0 reduce-scatter.5.cloned.1.call-start
  287.8 0.6 multiply_reduce_fusion.3
  288.4 0.7 fusion.8
  289.1 59.9 %all-reduce.2.cloned.1.call-done = bf16[2,64,2048]{2,1,0:T(8,128)(2,1)} async-done(((bf16[2,64,2048]{2,1,0:T(8,128)(2,1)}), bf16[2,64,2048]{2,1,0:T(8,128)(2,1)}) %all-reduce.2.cloned.1.call-update) | async-done | bytes 524304 | tf_op jit(solution)/shard_map/psum | solution.py:33
  349.0 5.3 fusion.3
  354.3 7.3 %convolution_convert_fusion.1 = bf16[128,4096]{1,0:T(8,128)(2,1)} fusion(bf16[128,1024]{1,0:T(8,128)(2,1)S(1)} %bitcast.24, bf16[4096,1024]{1,0:T(8,128)(2,1)} %all-gather.3.cloned.1.call-done), kind=kOutput, calls=%fused_computation.1 | convolution fusion | flops 1074266112 | bytes 9699328 | tf_op jit(solution)/shard_map/dot_general | solution.py:62
  361.6 0.0 reduce-scatter.5.cloned.1.call-update
  361.7 0.0 copy-start
  361.7 0.0 reduce-scatter.3.cloned.1.call-start
  361.7 5.6 convolution_convert_fusion
  367.3 0.0 reduce-scatter.3.cloned.1.call-update
  369.3 0.0 copy-done
  369.3 0.9 multiply_reduce_fusion
  370.8 77.3 %psum.31 = f32[]{:T(128)} all-reduce(f32[]{:T(128)S(6)} %add.33), channel_id=1, replica_groups=mesh['dp'=32,'feat'=8] {'dp','feat'}, use_global_device_ids=true, to_apply=%region_9.10 | all-reduce | flops 1 | bytes 8 | tf_op jit(solution)/shard_map/psum | solution.py:46
  448.2 0.0 reduce-scatter.5.cloned.1.call-done
  448.2 1.5 fusion.9
  449.7 182.3 %reduce-scatter.3.cloned.1.call-done = bf16[128,1024]{1,0:T(8,128)(2,1)} async-done(((bf16[4096,1024]{1,0:T(8,128)(2,1)}), bf16[128,1024]{1,0:T(8,128)(2,1)}) %reduce-scatter.3.cloned.1.call-update) | async-done | bytes 262160 | tf_op jit(solution)/shard_map/reduce_scatter | solution.py:70
  (3 shorter events, 0.1 us)
Async XLA Ops:
  7.2 104.1 %all-gather.3.cloned.1.call-start = ((), (), s32[]{:S(2)}) async-start(), calls=%async_computation.2 | async-start | bytes 8650752 | tf_op jit(solution)/shard_map/all_gather | solution.py:19
  7.9 272.9 %all-gather.5.cloned.1.call-start = ((), (), s32[]{:S(2)}) async-start(), calls=%async_computation.3 | async-start | bytes 8650752 | tf_op jit(solution)/shard_map/all_gather | solution.py:29
  189.1 159.9 %all-reduce.2.cloned.1.call-start = ((), (), s32[]{:S(2)}) async-start(), calls=%async_computation.4 | async-start | bytes 1048576 | tf_op jit(solution)/shard_map/psum | solution.py:33
  287.8 160.4 %reduce-scatter.5.cloned.1.call-start = ((), (), s32[]{:S(2)}) async-start(), calls=%async_computation.6 | async-start | bytes 1179648 | tf_op jit(solution)/shard_map/reduce_scatter | solution.py:65
  361.7 7.6 %copy-start = (bf16[2,64,2048]{2,1,0:T(8,128)(2,1)S(1)}, bf16[2,64,2048]{2,1,0:T(8,128)(2,1)}, u32[]{:S(2)}) copy-start(bf16[2,64,2048]{2,1,0:T(8,128)(2,1)} %all-reduce.2.cloned.1.call-done) | copy-start | bytes 1572868
  361.7 270.3 %reduce-scatter.3.cloned.1.call-start = ((), (), s32[]{:S(2)}) async-start(), calls=%async_computation.5 | async-start | bytes 8650752 | tf_op jit(solution)/shard_map/reduce_scatter | solution.py:70
Sparse Core Ops, SparseCore 0:
  10.6 100.6 all-gather.2
  189.2 91.5 all-gather.4
  287.9 61.1 all-reduce.1
  361.8 33.2 reduce-scatter.4
  399.5 232.4 reduce-scatter.2
where the time goes:
time: 639 us
  waiting for transfers between devices  339 us (53%)
  blocking collectives  249 us (39%)
  matrix products  29.8 us (5%)
  between operations  16.5 us (3%)
    reduce_scatter x1, waiting for transfers between devices, on_device(): lax.psum_scatter(lax.dot_general(stacked, flat_grads, (((0,), (0,)), ((),...  182 us
    psum x1, blocking collectives, on_device(): total_loss = lax.psum(local_share, ('dp', 'feat'))  77.3 us
    all_gather x1, waiting for transfers between devices, on_device(): whole_weight = lax.all_gather(weight, 'dp', axis=0, tiled=True)  76.4 us
    psum x1, blocking collectives, on_device(): col_sum = lax.psum(jnp.sum(views, axis=1), 'dp')  72.4 us
    psum x1, blocking collectives, on_device(): second_sum = lax.psum(jnp.sum(centered * centered, axis=1), 'dp')  72.3 us
    psum x1, waiting for transfers between devices, on_device(): lax.psum(gram_part.astype(jnp.bfloat16), 'feat').astype(jnp.float32)  59.9 us
    all_gather x1, waiting for transfers between devices, on_device(): gathered = lax.all_gather(centered_half, 'dp', axis=1, tiled=True)  19.3 us
    all_gather x1, blocking collectives, on_device(): lax.all_gather(hidden_first, 'feat', axis=1, tiled=True)  13.5 us
  transfers between devices with their start and end apart: 5, of which 4 were waited for; matrix products, arithmetic and copies ran while one was open for 1% of the time, Pallas kernels for 0%

commit v1 on v0

--- a/solution.py
+++ b/solution.py
@@ -16,7 +16,12 @@
         lax.all_gather(hidden_second, "feat", axis=1, tiled=True),
     )
     stacked = jnp.concatenate([full_first, full_second], axis=0)
-    whole_weight = lax.all_gather(weight, "dp", axis=0, tiled=True)
+    whole_weight = jnp.concatenate(
+        jax.lax.all_to_all(
+            jnp.stack([weight for _ in range(jax.lax.axis_size("dp"))], axis=0), "dp", 0, 0
+        ),
+        axis=0,
+    )
     outputs = jnp.dot(stacked, whole_weight, preferred_element_type=jnp.float32)
     views = outputs.reshape(2, row_count, col_count)
     col_sum = lax.psum(jnp.sum(views, axis=1), "dp")

time: 639 us -> 743 us (1.16)
  waiting for transfers between devices: 339 us -> 424 us
  starting transfers between devices: 0.2 us -> 11.9 us
    all_to_all x0 -> x1, waiting for transfers between devices: none -> 162 us  [on_device(): jax.lax.all_to_all(jnp.stack([weight for _ in range(jax.lax.axis_size('dp...]
    all_gather x1 -> x0, waiting for transfers between devices: 76.4 us -> none  [on_device(): whole_weight = lax.all_gather(weight, 'dp', axis=0, tiled=True)]
    all_to_all x0 -> x1, starting transfers between devices: none -> 11.6 us  [on_device(): jax.lax.all_to_all(jnp.stack([weight for _ in range(jax.lax.axis_size('dp...]
where the time goes in v1:
time: 743 us
  waiting for transfers between devices  424 us (57%)
  blocking collectives  250 us (34%)
  matrix products  29.8 us (4%)
  between operations  16.5 us (2%)
  starting transfers between devices  11.9 us (2%)
    reduce_scatter x1, waiting for transfers between devices, on_device(): lax.psum_scatter(lax.dot_general(stacked, flat_grads, (((0,), (0,)), ((),...  183 us
    all_to_all x1, waiting for transfers between devices, on_device(): jax.lax.all_to_all(jnp.stack([weight for _ in range(jax.lax.axis_size('dp...  162 us
    psum x1, blocking collectives, on_device(): total_loss = lax.psum(local_share, ('dp', 'feat'))  77.6 us
    psum x1, blocking collectives, on_device(): col_sum = lax.psum(jnp.sum(views, axis=1), 'dp')  74.1 us
    psum x1, blocking collectives, on_device(): second_sum = lax.psum(jnp.sum(centered * centered, axis=1), 'dp')  72 us
    psum x1, waiting for transfers between devices, on_device(): lax.psum(gram_part.astype(jnp.bfloat16), 'feat').astype(jnp.float32)  59.9 us
    all_gather x1, waiting for transfers between devices, on_device(): gathered = lax.all_gather(centered_half, 'dp', axis=1, tiled=True)  19.7 us
  transfers between devices with their start and end apart: 5, of which 4 were waited for; matrix products, arithmetic and copies ran while one was open for 1% of the time, Pallas kernels for 0%

profile of v1, /device:TPU:8, one launch (start us, length us, event | category | flops | bytes accessed | tf_op | source)
XLA Modules:
  0.0 742.5 jit_solution(17096508511477184984)
XLA Ops:
  7.2 5.2 stack.4
  12.4 0.0 copy-start.1
  12.4 0.0 copy-start.2
  12.4 11.6 %all-to-all-start = ((bf16[32,128,1024]{2,1,0:T(8,128)(2,1)}), bf16[32,128,1024]{2,1,0:T(8,128)(2,1)}, u32[]{:S(2)}, u32[]{:S(2)}) async-start(bf16[32,128,1024]{2,1,0:T(8,128)(2,1)} %stack.4), calls=%async_computation | async-start | bytes 16777216 | tf_op jit(solution)/shard_map/all_to_all | solution.py:20
  24.0 0.0 all-gather.2.cloned.1.call-start
  24.0 0.0 copy-done.1
  24.0 13.3 %all_gather.9 = bf16[64,4096]{1,0:T(8,128)(2,1)S(1)} all-gather(bf16[64,512]{1,0:T(8,128)(2,1)S(1)} %copy-done.1), channel_id=1, replica_groups=mesh['dp'=32,'feat'=8] {'feat'}, dimensions={1}, use_global_device_ids=true | all-gather | bytes 589824 | tf_op jit(solution)/shard_map/all_gather | solution.py:15
  37.4 0.0 copy-done.2
  37.4 13.1 %all_gather.10 = bf16[64,4096]{1,0:T(8,128)(2,1)S(1)} all-gather(bf16[64,512]{1,0:T(8,128)(2,1)S(1)} %copy-done.2), channel_id=1, replica_groups=mesh['dp'=32,'feat'=8] {'feat'}, dimensions={1}, use_global_device_ids=true | all-gather | bytes 589824 | tf_op jit(solution)/shard_map/all_gather | solution.py:16
  50.6 162.2 %all-to-all-done = bf16[32,128,1024]{2,1,0:T(8,128)(2,1)} async-done(((bf16[32,128,1024]{2,1,0:T(8,128)(2,1)}), bf16[32,128,1024]{2,1,0:T(8,128)(2,1)}, u32[]{:S(2)}, u32[]{:S(2)}) %all-to-all-start) | async-done | bytes 8388640 | tf_op jit(solution)/shard_map/all_to_all | solution.py:20
  212.8 4.6 bitcast_reduce_fusion
  217.4 74.1 %psum.28 = f32[2,1024]{1,0:T(2,128)S(1)} all-reduce(f32[2,1024]{1,0:T(2,128)S(1)} %get-tuple-element.15), channel_id=1, replica_groups=mesh['dp'=32,'feat'=8] {'dp'}, use_global_device_ids=true, to_apply=%region_2.0 | all-reduce | flops 2048 | bytes 16384 | tf_op jit(solution)/shard_map/psum | solution.py:27
  291.5 0.8 fusion.5
  292.3 0.0 all-gather.2.cloned.1.call-update
  292.3 0.0 all-reduce.2.cloned.1.call-start
  292.4 72.0 %psum.29 = f32[2,1024]{1,0:T(2,128)S(1)} all-reduce(f32[2,1024]{1,0:T(2,128)S(1)} %get-tuple-element.7), channel_id=1, replica_groups=mesh['dp'=32,'feat'=8] {'dp'}, use_global_device_ids=true, to_apply=%region_4.0 | all-reduce | flops 2048 | bytes 16384 | tf_op jit(solution)/shard_map/psum | solution.py:30
  364.4 19.7 %all-gather.2.cloned.1.call-done = bf16[2,2048,1024]{2,1,0:T(8,128)(2,1)} async-done(((bf16[2,64,1024]{2,1,0:T(8,128)(2,1)}), bf16[2,2048,1024]{2,1,0:T(8,128)(2,1)}) %all-gather.2.cloned.1.call-update) | async-done | bytes 8388624 | tf_op jit(solution)/shard_map/all_gather | solution.py:34
  384.1 6.9 convolution_convert_fusion.2
  391.0 0.0 all-reduce.2.cloned.1.call-update
  391.0 0.0 reduce-scatter.5.cloned.1.call-start
  391.1 0.6 multiply_reduce_fusion.3
  391.7 0.7 fusion.8
  392.4 59.9 %all-reduce.2.cloned.1.call-done = bf16[2,64,2048]{2,1,0:T(8,128)(2,1)} async-done(((bf16[2,64,2048]{2,1,0:T(8,128)(2,1)}), bf16[2,64,2048]{2,1,0:T(8,128)(2,1)}) %all-reduce.2.cloned.1.call-update) | async-done | bytes 524304 | tf_op jit(solution)/shard_map/psum | solution.py:38
  452.3 5.3 fusion.3
  457.6 7.3 convolution_convert_fusion.1
  464.9 0.0 reduce-scatter.5.cloned.1.call-update
  465.0 0.0 copy-start
  465.0 0.2 reduce-scatter.3.cloned.1.call-start
  465.2 5.6 convolution_convert_fusion
  470.8 0.0 reduce-scatter.3.cloned.1.call-update
  472.8 0.0 copy-done
  472.8 0.9 multiply_reduce_fusion
  474.3 77.6 %psum.31 = f32[]{:T(128)} all-reduce(f32[]{:T(128)S(6)} %add.33), channel_id=1, replica_groups=mesh['dp'=32,'feat'=8] {'dp','feat'}, use_global_device_ids=true, to_apply=%region_9.10 | all-reduce | flops 1 | bytes 8 | tf_op jit(solution)/shard_map/psum | solution.py:51
  551.9 0.0 reduce-scatter.5.cloned.1.call-done
  551.9 1.5 fusion.9
  553.4 182.6 %reduce-scatter.3.cloned.1.call-done = bf16[128,1024]{1,0:T(8,128)(2,1)} async-done(((bf16[4096,1024]{1,0:T(8,128)(2,1)}), bf16[128,1024]{1,0:T(8,128)(2,1)}) %reduce-scatter.3.cloned.1.call-update) | async-done | bytes 262160 | tf_op jit(solution)/shard_map/reduce_scatter | solution.py:75
  (3 shorter events, 0.1 us)
Async XLA Ops:
  12.4 11.6 %copy-start.1 = (bf16[64,512]{1,0:T(8,128)(2,1)S(1)}, bf16[64,512]{1,0:T(8,128)(2,1)}, u32[]{:S(2)}) copy-start(bf16[64,512]{1,0:T(8,128)(2,1)} %param.3) | copy-start | bytes 196612
  12.4 25.0 %copy-start.2 = (bf16[64,512]{1,0:T(8,128)(2,1)S(1)}, bf16[64,512]{1,0:T(8,128)(2,1)}, u32[]{:S(2)}) copy-start(bf16[64,512]{1,0:T(8,128)(2,1)} %param.4) | copy-start | bytes 196612
  12.4 200.4 %all-to-all-start = ((bf16[32,128,1024]{2,1,0:T(8,128)(2,1)}), bf16[32,128,1024]{2,1,0:T(8,128)(2,1)}, u32[]{:S(2)}, u32[]{:S(2)}) async-start(bf16[32,128,1024]{2,1,0:T(8,128)(2,1)} %stack.4), calls=%async_computation | async-start | bytes 16777216 | tf_op jit(solution)/shard_map/all_to_all | solution.py:20
  24.0 360.1 %all-gather.2.cloned.1.call-start = ((), (), s32[]{:S(2)}) async-start(), calls=%async_computation.3 | async-start | bytes 8650752 | tf_op jit(solution)/shard_map/all_gather | solution.py:34
  292.3 160.0 %all-reduce.2.cloned.1.call-start = ((), (), s32[]{:S(2)}) async-start(), calls=%async_computation.4 | async-start | bytes 1048576 | tf_op jit(solution)/shard_map/psum | solution.py:38
  391.0 160.8 %reduce-scatter.5.cloned.1.call-start = ((), (), s32[]{:S(2)}) async-start(), calls=%async_computation.6 | async-start | bytes 1179648 | tf_op jit(solution)/shard_map/reduce_scatter | solution.py:70
  465.0 7.8 %copy-start = (bf16[2,64,2048]{2,1,0:T(8,128)(2,1)S(1)}, bf16[2,64,2048]{2,1,0:T(8,128)(2,1)}, u32[]{:S(2)}) copy-start(bf16[2,64,2048]{2,1,0:T(8,128)(2,1)} %all-reduce.2.cloned.1.call-done) | copy-start | bytes 1572868
  465.0 271.0 %reduce-scatter.3.cloned.1.call-start = ((), (), s32[]{:S(2)}) async-start(), calls=%async_computation.5 | async-start | bytes 8650752 | tf_op jit(solution)/shard_map/reduce_scatter | solution.py:75
Sparse Core Ops, SparseCore 0:
  292.4 91.5 all-gather.1
  391.2 61.1 all-reduce.1
  465.1 33.3 reduce-scatter.4
  502.9 233.0 reduce-scatter.2
